TPU v7x, 32 devices: a whole 2x2x4 slice. The times are simulated.
32 devices in a mesh: leaf: 8 (over z, y), row: 4 (over x, core).
Axes of the slice: x: 2, y: 2, z: 4, core: 2. Of those that a mesh axis runs over, the one named last changes fastest.
Arguments:
- rhs_blocks: float32 [7, 1024, 256], P(None, 'leaf'), may hold values from -6 to 6
- diag_inverse: float32 [7, 1024, 1024], P(None, 'leaf', 'row'), may hold values from -0.1875 to 0.1875
- lower_blocks: float32 [6, 1024, 1024], P(None, 'leaf', 'row'), may hold values from -0.09375 to 0.09375
- update_rows: int32 [6, 1024], P(None, 'leaf'), may hold values from 512 to 895, as said below
Outputs:
- solution: float32 [7, 1024, 256], P(None, 'leaf')
Inputs may be any that keep to these rules, and one draw needn't show every extreme that they name: update_rows[s, m] = a * 128 + c names column i * 128 + c of an ancestor a of supernode s, where i = m // 128; the 128 entries of one supernode with the same i are distinct.
All inputs are finite; a program needn't handle non-finite values.
Results may differ from a plain program's by a relative error of at most 0.0001.
Values sent between devices are 32-bit elements; how exact they have to be, the bound alone decides.
No kernel may reach another device: no remote copies, remote signals or barrier semaphores. Data moves between devices by JAX's collectives and lax.ppermute only.
A program may use at most 64 MiB of HBM per device.

v0:
```python
import jax
import jax.numpy as jnp
from jax import lax
from jax.sharding import PartitionSpec as P


def local(rhs_blocks, diag_inverse, lower_blocks, update_rows):
    leaf_count = lax.axis_size("leaf")
    node_total = rhs_blocks.shape[0]
    panel_rows = rhs_blocks.shape[1]
    rhs_width = rhs_blocks.shape[2]
    level_total = (node_total + 1).bit_length() - 1
    slice_rows = diag_inverse.shape[2] // leaf_count
    current = rhs_blocks.reshape(node_total * panel_rows, rhs_width)
    stored_slices = [None] * level_total
    for depth_level in range(level_total - 1, -1, -1):
        first_node = 2**level_total - 2 ** (depth_level + 1)
        node_count = 2**depth_level
        stop_node = first_node + node_count
        diag_part = diag_inverse[first_node:stop_node]
        lower_part = lower_blocks[first_node:stop_node] if depth_level > 0 else None
        local_rhs = current[first_node * panel_rows : stop_node * panel_rows].reshape(
            node_count, panel_rows, rhs_width
        )
        partial_value = jnp.einsum(
            "scr,sct->rst", diag_part, local_rhs, precision=lax.Precision.HIGHEST
        )
        complete = lax.psum(partial_value, "leaf")
        stored = lax.dynamic_slice_in_dim(
            complete, lax.axis_index("leaf") * slice_rows, slice_rows, 0
        )
        if depth_level > 0:
            update = jnp.einsum(
                "smr,rst->smt", lower_part, complete, precision=lax.Precision.HIGHEST
            )
        stored_slices[depth_level] = stored
        if depth_level > 0:
            update = lax.psum(update, "row")
            targets = update_rows[first_node:stop_node].reshape(-1)
            current = current.at[targets].add(-update.reshape(-1, rhs_width))
    answer = jnp.zeros((node_total * panel_rows, rhs_width), jnp.float32)
    for depth_level in range(level_total):
        first_node = 2**level_total - 2 ** (depth_level + 1)
        node_count = 2**depth_level
        stop_node = first_node + node_count
        diag_part = diag_inverse[first_node:stop_node]
        residual = stored_slices[depth_level]
        if depth_level > 0:
            lower_part = lower_blocks[first_node:stop_node]
            targets = update_rows[first_node:stop_node].reshape(-1)
            known = answer[targets].reshape(node_count, panel_rows, rhs_width)
            residual = residual - lax.psum_scatter(
                jnp.einsum("smr,smt->rst", lower_part, known, precision=lax.Precision.HIGHEST),
                "leaf",
                scatter_dimension=0,
                tiled=True,
            )
        partial_value = jnp.einsum(
            "scr,rst->sct",
            diag_part,
            lax.all_gather(residual, "leaf", axis=0, tiled=True),
            precision=lax.Precision.HIGHEST,
        )
        solved = lax.psum(partial_value, "row")
        answer = answer.at[first_node * panel_rows : stop_node * panel_rows].set(
            solved.reshape(-1, rhs_width)
        )
    return answer.reshape(node_total, panel_rows, rhs_width)


def solution(mesh):
    placed = (
        P(None, "leaf", None),
        P(None, "leaf", "row"),
        P(None, "leaf", "row"),
        P(None, "leaf"),
    )
    return jax.shard_map(
        local, mesh=mesh, in_specs=placed, out_specs=P(None, "leaf", None), check_vma=False
    )
```

profile of v0, /device:TPU:0, one launch (start us, length us, event | category | flops | bytes accessed | tf_op | source)
XLA Modules:
  0.0 698.2 jit_solution(705623157416841822)
XLA Ops:
  6.5 1.3 copy.104
  8.0 2.0 convolution_bitcast_fusion.1
  10.1 81.5 %all-reduce.14.cloned.1.call-done = f32[256,4,256]{2,0,1:T(8,128)} async-done(((f32[256,4,256]{2,0,1:T(8,128)}), f32[256,4,256]{2,0,1:T(8,128)}) %all-reduce.14.cloned.1.call-update) | async-done | bytes 1048592 | tf_op jit(solution)/shard_map/psum | solution.py:28
  91.6 3.9 convolution_bitcast_fusion.4
  96.2 32.2 %all-reduce.16.cloned.1.call-done = f32[4,128,256]{1,2,0:T(8,128)} async-done(((f32[4,128,256]{1,2,0:T(8,128)}), f32[4,128,256]{1,2,0:T(8,128)}) %all-reduce.16.cloned.1.call-update) | async-done | bytes 524304 | tf_op jit(solution)/shard_map/psum | solution.py:38
  128.4 1.9 neg.12
  130.3 1.2 copy.47
  131.6 3.7 scatter_fusion
  135.3 1.4 convolution_bitcast_fusion.3
  137.4 71.9 %all-reduce.18.cloned.1.call-done = f32[256,2,256]{2,0,1:T(8,128)} async-done(((f32[256,2,256]{2,0,1:T(8,128)}), f32[256,2,256]{2,0,1:T(8,128)}) %all-reduce.18.cloned.1.call-update) | async-done | bytes 524304 | tf_op jit(solution)/shard_map/psum | solution.py:28
  209.3 2.8 convolution_bitcast_fusion.5
  212.1 31.3 %all-reduce.20.cloned.1.call-done = f32[2,128,256]{1,2,0:T(8,128)} async-done(((f32[2,128,256]{1,2,0:T(8,128)}), f32[2,128,256]{1,2,0:T(8,128)}) %all-reduce.20.cloned.1.call-update) | async-done | bytes 262160 | tf_op jit(solution)/shard_map/psum | solution.py:38
  244.6 2.3 scatter_fusion.1
  246.9 1.1 convolution_bitcast_fusion.6
  248.1 70.6 %all-reduce.22.cloned.1.call-done = f32[256,1,256]{0,2,1:T(8,128)} async-done(((f32[256,1,256]{0,2,1:T(8,128)}), f32[256,1,256]{0,2,1:T(8,128)}) %all-reduce.22.cloned.1.call-update) | async-done | bytes 262160 | tf_op jit(solution)/shard_map/psum | solution.py:28
  319.8 30.8 %all_gather.9 = f32[256,1,256]{2,1,0:T(1,128)S(1)} all-gather(f32[32,1,256]{2,1,0:T(1,128)S(1)} %copy.52), channel_id=1, replica_groups=mesh['leaf'=8,'row'=4] {'leaf'}, dimensions={0}, use_global_device_ids=true | all-gather | bytes 294912 | tf_op jit(solution)/shard_map/all_gather | solution.py:61
  350.6 1.3 convolution_bitcast_fusion.7
  352.0 30.8 %all-reduce.24.cloned.1.call-done = f32[128,256]{0,1:T(8,128)} async-done(((f32[128,256]{0,1:T(8,128)}), f32[128,256]{0,1:T(8,128)}) %all-reduce.24.cloned.1.call-update) | async-done | bytes 131088 | tf_op jit(solution)/shard_map/psum | solution.py:64
  384.1 1.7 gather_fusion
  385.7 1.6 convolution_bitcast_fusion.2
  390.3 70.6 %all-reduce.30.cloned.1.call-done = f32[256,2,256]{2,1,0:T(2,128)} async-done(((f32[256,2,256]{2,1,0:T(2,128)}), f32[256,2,256]{2,1,0:T(2,128)}) %all-reduce.30.cloned.1.call-update) | async-done | bytes 524304
  462.6 31.8 %all_gather.10 = f32[256,2,256]{2,1,0:T(2,128)S(1)} all-gather(f32[32,2,256]{2,1,0:T(2,128)S(1)} %copy.57), channel_id=1, replica_groups=mesh['leaf'=8,'row'=4] {'leaf'}, dimensions={0}, use_global_device_ids=true | all-gather | bytes 589824 | tf_op jit(solution)/shard_map/all_gather | solution.py:61
  495.8 31.2 %all-reduce.26.cloned.1.call-done = f32[256,256]{0,1:T(8,128)} async-done(((f32[256,256]{0,1:T(8,128)}), f32[256,256]{0,1:T(8,128)}) %all-reduce.26.cloned.1.call-update) | async-done | bytes 262160 | tf_op jit(solution)/shard_map/psum | solution.py:64
  528.3 1.6 gather_fusion.1
  529.8 2.1 convolution_bitcast_fusion
  531.9 1.3 copy.62
  533.3 78.3 %all-reduce.32.cloned.1.call-done = f32[256,4,256]{2,1,0:T(4,128)} async-done(((f32[256,4,256]{2,1,0:T(4,128)}), f32[256,4,256]{2,1,0:T(4,128)}) %all-reduce.32.cloned.1.call-update) | async-done | bytes 1048592
  614.3 39.8 %all-gather.2.cloned.1.call-done = f32[256,4,256]{2,1,0:T(4,128)} async-done(((f32[32,4,256]{2,1,0:T(4,128)}), f32[256,4,256]{2,1,0:T(4,128)}) %all-gather.2.cloned.1.call-update) | async-done | bytes 1048592 | tf_op jit(solution)/shard_map/all_gather | solution.py:61
  654.1 2.1 fusion
  657.3 32.1 %all-reduce.28.cloned.1.call-done = f32[512,256]{0,1:T(8,128)} async-done(((f32[512,256]{0,1:T(8,128)}), f32[512,256]{0,1:T(8,128)}) %all-reduce.28.cloned.1.call-update) | async-done | bytes 524304 | tf_op jit(solution)/shard_map/psum | solution.py:64
  689.3 1.1 constant_dynamic-update-slice_fusion
  690.4 1.2 copy.67
  (59 shorter events, 15.7 us)
Async XLA Ops:
  6.5 1.5 copy-start
  6.5 85.1 %all-reduce.14.cloned.1.call-start = ((), (), s32[]{:S(2)}) async-start(), calls=%async_computation | async-start | bytes 2097152 | tf_op jit(solution)/shard_map/psum | solution.py:28
  10.0 81.6 %copy-start.2 = (f32[6,128,256]{2,1,0:T(8,128)S(1)}, f32[6,128,256]{2,1,0:T(8,128)}, u32[]{:S(2)}) copy-start(f32[6,128,256]{2,1,0:T(8,128)} %param.12) | copy-start | bytes 2359300
  10.1 118.4 %all-reduce.16.cloned.1.call-start = ((), (), s32[]{:S(2)}) async-start(), calls=%async_computation.1 | async-start | bytes 1048576 | tf_op jit(solution)/shard_map/psum | solution.py:38
  95.5 0.7 slice-start
  95.5 113.7 %all-reduce.18.cloned.1.call-start = ((), (), s32[]{:S(2)}) async-start(), calls=%async_computation.2 | async-start | bytes 1048576 | tf_op jit(solution)/shard_map/psum | solution.py:28
  136.7 0.7 copy-start.3
  136.7 106.8 %all-reduce.20.cloned.1.call-start = ((), (), s32[]{:S(2)}) async-start(), calls=%async_computation.3 | async-start | bytes 524288 | tf_op jit(solution)/shard_map/psum | solution.py:38
  212.1 106.7 %all-reduce.22.cloned.1.call-start = ((), (), s32[]{:S(2)}) async-start(), calls=%async_computation.4 | async-start | bytes 524288 | tf_op jit(solution)/shard_map/psum | solution.py:28
  248.0 134.7 %all-reduce.24.cloned.1.call-start = ((), (), s32[]{:S(2)}) async-start(), calls=%async_computation.5 | async-start | bytes 262144 | tf_op jit(solution)/shard_map/psum | solution.py:64
  351.9 108.9 %all-reduce.30.cloned.1.call-start = ((), (), s32[]{:S(2)}) async-start(), calls=%async_computation.9 | async-start | bytes 1048576
  388.3 138.7 %all-reduce.26.cloned.1.call-start = ((), (), s32[]{:S(2)}) async-start(), calls=%async_computation.6 | async-start | bytes 524288 | tf_op jit(solution)/shard_map/psum | solution.py:64
  388.4 0.7 copy-start.4
  495.7 115.9 %all-reduce.32.cloned.1.call-start = ((), (), s32[]{:S(2)}) async-start(), calls=%async_computation.10 | async-start | bytes 2097152
  533.2 120.9 %copy-start.1 = (f32[7,128,256]{2,1,0:T(8,128)S(1)}, f32[7,128,256]{2,1,0:T(8,128)}, u32[]{:S(2)}) copy-start(f32[7,128,256]{2,1,0:T(8,128)} %param.11) | copy-start | bytes 2752516
  533.3 120.9 %all-gather.2.cloned.1.call-start = ((), (), s32[]{:S(2)}) async-start(), calls=%async_computation.7 | async-start | bytes 1179648 | tf_op jit(solution)/shard_map/all_gather | solution.py:61
  614.2 75.1 %all-reduce.28.cloned.1.call-start = ((), (), s32[]{:S(2)}) async-start(), calls=%async_computation.8 | async-start | bytes 1048576 | tf_op jit(solution)/shard_map/psum | solution.py:64
Sparse Core Ops, SparseCore 0:
  10.9 80.7 all-reduce.13
  95.6 32.7 all-reduce.15
  136.8 72.3 all-reduce.17
  212.2 31.2 all-reduce.19
  248.2 70.5 all-reduce.21
  352.0 30.6 all-reduce.23
  388.4 72.3 all-reduce.29
  495.8 31.1 all-reduce.25
  533.4 78.1 all-reduce.31
  614.4 39.7 all-gather.1
  657.4 31.8 all-reduce.27
where the time goes:
time: 699 us; the launch traced here: 698 us
  waiting for transfers between devices  571 us (82%)
  blocking collectives  62.6 us (9%)
  local copies, waits for them, and re-layouts  21.2 us (3%)
  matrix products  18.7 us (3%)
  between operations  14.1 us (2%)
  other arithmetic  10.6 us (2%)
    psum x3, waiting for transfers between devices, local(): complete = lax.psum(partial_value, 'leaf')  224 us
    unnamed x13, waiting for transfers between devices  149 us
    psum x3, waiting for transfers between devices, local(): solved = lax.psum(partial_value, 'row')  94.1 us
    psum x2, waiting for transfers between devices, local(): update = lax.psum(update, 'row')  63.6 us
    all_gather x2, blocking collectives, local(): lax.all_gather(residual, 'leaf', axis=0, tiled=True)  62.6 us
    all_gather x1, waiting for transfers between devices, local(): lax.all_gather(residual, 'leaf', axis=0, tiled=True)  39.8 us
  transfers between devices with their start and end apart: 11, of which 11 were waited for; matrix products, arithmetic and copies ran while one was open for 0% of the time, Pallas kernels for 0%

commit v1 on v0

--- a/solution.py
+++ b/solution.py
@@ -2,6 +2,18 @@
 import jax.numpy as jnp
 from jax import lax
 from jax.sharding import PartitionSpec as P
+
+
+def gather_by_bits(shard, axis, dim):
+    ways, here = (lax.axis_size(axis), lax.axis_index(axis))
+    grown, reach = (shard, 1)
+    while reach < ways:
+        theirs = lax.ppermute(grown, axis, [(d, d ^ reach) for d in range(ways)])
+        mine_first = jnp.concatenate([grown, theirs], axis=dim)
+        theirs_first = jnp.concatenate([theirs, grown], axis=dim)
+        grown = jnp.where(here & reach == 0, mine_first, theirs_first)
+        reach = 2 * reach
+    return grown
 
 
 def local(rhs_blocks, diag_inverse, lower_blocks, update_rows):
@@ -58,7 +70,7 @@
         partial_value = jnp.einsum(
             "scr,rst->sct",
             diag_part,
-            lax.all_gather(residual, "leaf", axis=0, tiled=True),
+            gather_by_bits(residual, "leaf", 0),
             precision=lax.Precision.HIGHEST,
         )
         solved = lax.psum(partial_value, "row")

time: 699 us -> 683 us (0.977)
  blocking collectives: 62.6 us -> 0 us
  waiting for transfers between devices: 571 us -> 611 us
  starting transfers between devices: 0.42 us -> 12.6 us
    ppermute x0 -> x9, waiting for transfers between devices: none -> 78 us  [gather_by_bits(): theirs = lax.ppermute(grown, axis, [(d, d ^ reach) for d in range(ways)])]
    all_gather x2 -> x0, blocking collectives: 62.6 us -> none  [local(): lax.all_gather(residual, 'leaf', axis=0, tiled=True)]
    all_gather x1 -> x0, waiting for transfers between devices: 39.8 us -> none  [local(): lax.all_gather(residual, 'leaf', axis=0, tiled=True)]
    ppermute x0 -> x9, starting transfers between devices: none -> 12.1 us  [gather_by_bits(): theirs = lax.ppermute(grown, axis, [(d, d ^ reach) for d in range(ways)])]
    unnamed x13 -> x12, waiting for transfers between devices: 149 us -> 149 us
  transfers between devices with their start and end apart: 11 -> 19, of which waited for: 11 -> 19; matrix products, arithmetic and copies ran while one was open for 0% -> 0% of each run, Pallas kernels for 0% -> 0%
where the time goes in v1:
time: 683 us
  waiting for transfers between devices  611 us (89%)
  local copies, waits for them, and re-layouts  19.1 us (3%)
  matrix products  15.6 us (2%)
  between operations  14.5 us (2%)
  starting transfers between devices  12.6 us (2%)
  other arithmetic  10 us (1%)
    psum x3, waiting for transfers between devices, local(): complete = lax.psum(partial_value, 'leaf')  224 us
    unnamed x12, waiting for transfers between devices  149 us
    psum x3, waiting for transfers between devices, local(): solved = lax.psum(partial_value, 'row')  96.3 us
    ppermute x9, waiting for transfers between devices, gather_by_bits(): theirs = lax.ppermute(grown, axis, [(d, d ^ reach) for d in range(ways)])  78 us
    psum x2, waiting for transfers between devices, local(): update = lax.psum(update, 'row')  63.6 us
  transfers between devices with their start and end apart: 19, of which 19 were waited for; matrix products, arithmetic and copies ran while one was open for 0% of the time, Pallas kernels for 0%

profile of v1, /device:TPU:0, one launch (start us, length us, event | category | flops | bytes accessed | tf_op | source)
XLA Modules:
  0.0 682.6 jit_solution(10572973923042864874)
XLA Ops:
  8.0 2.0 convolution_bitcast_fusion.1
  10.1 81.5 %all-reduce.14.cloned.1.call-done = f32[256,4,256]{0,2,1:T(8,128)} async-done(((f32[256,4,256]{0,2,1:T(8,128)}), f32[256,4,256]{0,2,1:T(8,128)}) %all-reduce.14.cloned.1.call-update) | async-done | bytes 1048592 | tf_op jit(solution)/shard_map/psum | solution.py:40
  91.6 3.1 convolution_bitcast_fusion.4
  95.4 32.2 %all-reduce.16.cloned.1.call-done = f32[4,128,256]{1,2,0:T(8,128)} async-done(((f32[4,128,256]{1,2,0:T(8,128)}), f32[4,128,256]{1,2,0:T(8,128)}) %all-reduce.16.cloned.1.call-update) | async-done | bytes 524304 | tf_op jit(solution)/shard_map/psum | solution.py:50
  128.9 3.7 scatter_fusion
  132.7 1.4 convolution_bitcast_fusion.3
  134.8 71.9 %all-reduce.18.cloned.1.call-done = f32[256,2,256]{0,2,1:T(8,128)} async-done(((f32[256,2,256]{0,2,1:T(8,128)}), f32[256,2,256]{0,2,1:T(8,128)}) %all-reduce.18.cloned.1.call-update) | async-done | bytes 524304 | tf_op jit(solution)/shard_map/psum | solution.py:40
  206.7 2.3 convolution_bitcast_fusion.5
  209.1 31.3 %all-reduce.20.cloned.1.call-done = f32[2,128,256]{1,2,0:T(8,128)} async-done(((f32[2,128,256]{1,2,0:T(8,128)}), f32[2,128,256]{1,2,0:T(8,128)}) %all-reduce.20.cloned.1.call-update) | async-done | bytes 262160 | tf_op jit(solution)/shard_map/psum | solution.py:50
  241.5 2.3 scatter_fusion.1
  245.1 70.6 %all-reduce.22.cloned.1.call-done = f32[256,1,256]{0,2,1:T(8,128)} async-done(((f32[256,1,256]{0,2,1:T(8,128)}), f32[256,1,256]{0,2,1:T(8,128)}) %all-reduce.22.cloned.1.call-update) | async-done | bytes 262160 | tf_op jit(solution)/shard_map/psum | solution.py:40
  317.7 4.1 collective-permute-done
  323.2 4.4 collective-permute-done.1
  327.7 2.4 collective-permute-start.2
  330.3 4.8 collective-permute-done.2
  336.2 31.5 %all-reduce.24.cloned.1.call-done = f32[128,256]{0,1:T(8,128)} async-done(((f32[128,256]{0,1:T(8,128)}), f32[128,256]{0,1:T(8,128)}) %all-reduce.24.cloned.1.call-update) | async-done | bytes 131088 | tf_op jit(solution)/shard_map/psum | solution.py:76
  373.7 70.4 %all-reduce.30.cloned.1.call-done = f32[256,2,256]{2,1,0:T(2,128)} async-done(((f32[256,2,256]{2,1,0:T(2,128)}), f32[256,2,256]{2,1,0:T(2,128)}) %all-reduce.30.cloned.1.call-update) | async-done | bytes 524304
  446.3 5.5 collective-permute-done.3
  453.0 6.5 collective-permute-done.4
  459.7 1.6 collective-permute-start.5
  461.3 8.6 %collective-permute-done.5 = f32[128,2,256]{0,2,1:T(8,128)S(1)} collective-permute-done((f32[128,2,256]{0,2,1:T(8,128)S(1)}, f32[128,2,256]{0,2,1:T(8,128)S(1)}, u32[]{:S(2)}, u32[]{:S(2)}) %collective-permute-start.5) | collective-permute-done | bytes 262176 | tf_op jit(solution)/shard_map/ppermute | solution.py:11
  469.8 1.7 fusion.6
  472.4 31.5 %all-reduce.26.cloned.1.call-done = f32[256,256]{0,1:T(8,128)} async-done(((f32[256,256]{0,1:T(8,128)}), f32[256,256]{0,1:T(8,128)}) %all-reduce.26.cloned.1.call-update) | async-done | bytes 262160 | tf_op jit(solution)/shard_map/psum | solution.py:76
  505.2 1.6 gather_fusion.1
  507.8 1.3 copy.40
  509.2 78.2 %all-reduce.32.cloned.1.call-done = f32[256,4,256]{2,1,0:T(4,128)} async-done(((f32[256,4,256]{2,1,0:T(4,128)}), f32[256,4,256]{2,1,0:T(4,128)}) %all-reduce.32.cloned.1.call-update) | async-done | bytes 1048592
  588.8 1.3 collective-permute-start.6
  590.1 11.7 %collective-permute-done.6 = f32[32,4,256]{0,2,1:T(8,128)S(1)} collective-permute-done((f32[32,4,256]{0,2,1:T(8,128)S(1)}, f32[32,4,256]{0,2,1:T(8,128)S(1)}, u32[]{:S(2)}, u32[]{:S(2)}) %collective-permute-start.6) | collective-permute-done | bytes 131104 | tf_op jit(solution)/shard_map/ppermute | solution.py:11
  602.9 11.4 %collective-permute-done.7 = f32[64,4,256]{0,2,1:T(8,128)S(1)} collective-permute-done((f32[64,4,256]{0,2,1:T(8,128)S(1)}, f32[64,4,256]{0,2,1:T(8,128)S(1)}, u32[]{:S(2)}, u32[]{:S(2)}) %collective-permute-start.7) | collective-permute-done | bytes 262176 | tf_op jit(solution)/shard_map/ppermute | solution.py:11
  614.6 2.1 collective-permute-start.8
  616.7 21.1 %collective-permute-done.8 = f32[128,4,256]{0,2,1:T(8,128)S(1)} collective-permute-done((f32[128,4,256]{0,2,1:T(8,128)S(1)}, f32[128,4,256]{0,2,1:T(8,128)S(1)}, u32[]{:S(2)}, u32[]{:S(2)}) %collective-permute-start.8) | collective-permute-done | bytes 524320 | tf_op jit(solution)/shard_map/ppermute | solution.py:11
  640.1 33.3 %all-reduce.28.cloned.1.call-done = f32[512,256]{0,1:T(8,128)} async-done(((f32[512,256]{0,1:T(8,128)}), f32[512,256]{0,1:T(8,128)}) %all-reduce.28.cloned.1.call-update) | async-done | bytes 524304 | tf_op jit(solution)/shard_map/psum | solution.py:76
  (88 shorter events, 30.7 us)
Async XLA Ops:
  6.5 1.5 copy-start.3
  6.5 85.1 %all-reduce.14.cloned.1.call-start = ((), (), s32[]{:S(2)}) async-start(), calls=%async_computation | async-start | bytes 2097152 | tf_op jit(solution)/shard_map/psum | solution.py:40
  10.0 81.6 %copy-start = (f32[6,128,256]{2,1,0:T(8,128)S(1)}, f32[6,128,256]{2,1,0:T(8,128)}, u32[]{:S(2)}) copy-start(f32[6,128,256]{2,1,0:T(8,128)} %param.12) | copy-start | bytes 2359300
  10.0 117.6 %all-reduce.16.cloned.1.call-start = ((), (), s32[]{:S(2)}) async-start(), calls=%async_computation.1 | async-start | bytes 1048576 | tf_op jit(solution)/shard_map/psum | solution.py:50
  94.7 0.7 slice-start
  94.7 111.9 %all-reduce.18.cloned.1.call-start = ((), (), s32[]{:S(2)}) async-start(), calls=%async_computation.2 | async-start | bytes 1048576 | tf_op jit(solution)/shard_map/psum | solution.py:40
  128.9 3.7 copy-start.4
  134.1 0.7 copy-start.7
  134.1 106.3 %all-reduce.20.cloned.1.call-start = ((), (), s32[]{:S(2)}) async-start(), calls=%async_computation.3 | async-start | bytes 524288 | tf_op jit(solution)/shard_map/psum | solution.py:50
  209.0 106.7 %all-reduce.22.cloned.1.call-start = ((), (), s32[]{:S(2)}) async-start(), calls=%async_computation.4 | async-start | bytes 524288 | tf_op jit(solution)/shard_map/psum | solution.py:40
  245.0 122.7 %all-reduce.24.cloned.1.call-start = ((), (), s32[]{:S(2)}) async-start(), calls=%async_computation.5 | async-start | bytes 262144 | tf_op jit(solution)/shard_map/psum | solution.py:76
  315.7 1.9 copy-start.6
  316.8 5.0 collective-permute-start
  322.0 5.6 collective-permute-start.1
  327.7 7.3 %collective-permute-start.2 = (f32[128,1,256]{0,2,1:T(8,128)S(1)}, f32[128,1,256]{0,2,1:T(8,128)S(1)}, u32[]{:S(2)}, u32[]{:S(2)}) collective-permute-start(f32[128,1,256]{0,2,1:T(8,128)S(1)} %maximum_select_fusion.13), channel_id=1, source_target_pairs={{0,16},{4,20},{8,24},{12,28},{16,0},{20,4},{24,8},{28,12},{1,17},{... | collective-permute-start | bytes 393224 | tf_op jit(solution)/shard_map/ppermute | solution.py:11
  336.1 108.0 %all-reduce.30.cloned.1.call-start = ((), (), s32[]{:S(2)}) async-start(), calls=%async_computation.8 | async-start | bytes 1048576
  371.6 73.6 %copy-start.2 = (f32[256,2,256]{0,2,1:T(8,128)S(1)}, f32[256,2,256]{0,2,1:T(8,128)}, u32[]{:S(2)}) copy-start(f32[256,2,256]{0,2,1:T(8,128)} %all-reduce.18.cloned.1.call-done) | copy-start | bytes 1572868
  371.6 132.3 %all-reduce.26.cloned.1.call-start = ((), (), s32[]{:S(2)}) async-start(), calls=%async_computation.6 | async-start | bytes 524288 | tf_op jit(solution)/shard_map/psum | solution.py:76
  371.9 0.7 copy-start.8
  445.3 6.4 collective-permute-start.3
  452.0 7.5 %collective-permute-start.4 = (f32[64,2,256]{0,2,1:T(8,128)S(1)}, f32[64,2,256]{0,2,1:T(8,128)S(1)}, u32[]{:S(2)}, u32[]{:S(2)}) collective-permute-start(f32[64,2,256]{0,2,1:T(8,128)S(1)} %maximum_select_fusion.8), channel_id=1, source_target_pairs={{0,8},{4,12},{8,0},{12,4},{16,24},{20,28},{24,16},{28,20},{1,9},{5... | collective-permute-start | bytes 393224 | tf_op jit(solution)/shard_map/ppermute | solution.py:11
  459.7 10.1 %collective-permute-start.5 = (f32[128,2,256]{0,2,1:T(8,128)S(1)}, f32[128,2,256]{0,2,1:T(8,128)S(1)}, u32[]{:S(2)}, u32[]{:S(2)}) collective-permute-start(f32[128,2,256]{0,2,1:T(8,128)S(1)} %maximum_select_fusion.9), channel_id=1, source_target_pairs={{0,16},{4,20},{8,24},{12,28},{16,0},{20,4},{24,8},{28,12},{1,17},{... | collective-permute-start | bytes 786440 | tf_op jit(solution)/shard_map/ppermute | solution.py:11
  472.4 115.1 %all-reduce.32.cloned.1.call-start = ((), (), s32[]{:S(2)}) async-start(), calls=%async_computation.9 | async-start | bytes 2097152
  509.1 79.4 %copy-start.1 = (f32[256,4,256]{0,2,1:T(8,128)S(1)}, f32[256,4,256]{0,2,1:T(8,128)}, u32[]{:S(2)}) copy-start(f32[256,4,256]{0,2,1:T(8,128)} %all-reduce.14.cloned.1.call-done) | copy-start | bytes 3145732
  509.1 164.3 %all-reduce.28.cloned.1.call-start = ((), (), s32[]{:S(2)}) async-start(), calls=%async_computation.7 | async-start | bytes 1048576 | tf_op jit(solution)/shard_map/psum | solution.py:76
  588.8 13.0 %collective-permute-start.6 = (f32[32,4,256]{0,2,1:T(8,128)S(1)}, f32[32,4,256]{0,2,1:T(8,128)S(1)}, u32[]{:S(2)}, u32[]{:S(2)}) collective-permute-start(f32[32,4,256]{0,2,1:T(8,128)S(1)} %dynamic-slice_subtract_fusion), channel_id=1, source_target_pairs={{0,4},{4,0},{8,12},{12,8},{16,20},{20,16},{24,28},{28,24},{1,5},{5... | collective-permute-start | bytes 393224 | tf_op jit(solution)/shard_map/ppermute | solution.py:11
  602.2 35.7 %copy-start.5 = (f32[7,128,256]{2,1,0:T(8,128)S(1)}, f32[7,128,256]{2,1,0:T(8,128)}, u32[]{:S(2)}) copy-start(f32[7,128,256]{2,1,0:T(8,128)} %param.11) | copy-start | bytes 2752516
  602.2 12.1 %collective-permute-start.7 = (f32[64,4,256]{0,2,1:T(8,128)S(1)}, f32[64,4,256]{0,2,1:T(8,128)S(1)}, u32[]{:S(2)}, u32[]{:S(2)}) collective-permute-start(f32[64,4,256]{0,2,1:T(8,128)S(1)} %maximum_select_fusion.4), channel_id=1, source_target_pairs={{0,8},{4,12},{8,0},{12,4},{16,24},{20,28},{24,16},{28,20},{1,9},{5... | collective-permute-start | bytes 786440 | tf_op jit(solution)/shard_map/ppermute | solution.py:11
  614.6 23.2 %collective-permute-start.8 = (f32[128,4,256]{0,2,1:T(8,128)S(1)}, f32[128,4,256]{0,2,1:T(8,128)S(1)}, u32[]{:S(2)}, u32[]{:S(2)}) collective-permute-start(f32[128,4,256]{0,2,1:T(8,128)S(1)} %maximum_select_fusion.5), channel_id=1, source_target_pairs={{0,16},{4,20},{8,24},{12,28},{16,0},{20,4},{24,8},{28,12},{1,17},{... | collective-permute-start | bytes 1572872 | tf_op jit(solution)/shard_map/ppermute | solution.py:11
Sparse Core Ops, SparseCore 0:
  10.9 80.7 all-reduce.13
  94.8 32.7 all-reduce.15
  134.2 72.3 all-reduce.17
  209.2 31.2 all-reduce.19
  245.1 70.5 all-reduce.21
  336.2 31.4 all-reduce.23
  371.8 72.3 all-reduce.29
  472.5 31.3 all-reduce.25
  509.3 78.1 all-reduce.31
  640.3 33.1 all-reduce.27
